TPU v7x, 256 devices: a whole 4x4x8 slice. The times are simulated.
256 devices in a mesh: dp: 64 (over z, x, core), section: 4 (over y).
Axes of the slice: x: 4, y: 4, z: 8, core: 2. Of those that a mesh axis runs over, the one named last changes fastest.
Arguments:
- token_ids: int32 [4, 64, 128], P('section', 'dp'), may hold values from 0 to 511
- segment_ids: int32 [4, 64, 128], P('section', 'dp'), may hold values from 0 to 3, never falling along the last dimension, each value on 1 to 64 neighbouring positions
- row_order: int32 [4, 64], P('section', 'dp'), may hold values from 0 to 63, each once within a row
- embed_table: bfloat16 [4, 512, 4096], P('section'), may hold values from -6 to 6
- norm_gain: float32 [4, 4096], P('section'), may hold values from 0.5 to 2
- position_bias: float32 [4, 32, 64], P('section'), may hold values from -4 to 4
- returned_grad: bfloat16 [4, 8192, 4096], P('section', 'dp'), may hold values from -6 to 6
Outputs:
- handed: bfloat16 [4, 8192, 4096], P('section', 'dp')
- grad_table: float32 [4, 512, 4096], P('section', 'dp')
- grad_gain: float32 [4, 4096], P('section')
- grad_bias: float32 [4, 32, 64], P('section')
All inputs are finite; a program needn't handle non-finite values.
Results may differ from a plain program's by a relative error of at most 0.014.
Values may be sent and summed in bfloat16 or wider, within the bound.
No kernel may reach another device: no remote copies, remote signals or barrier semaphores. Data moves between devices by JAX's collectives and lax.ppermute only.
A program may use at most 128 MiB of HBM per device.

v0:
```python
import jax
import jax.numpy as jnp
from jax import lax
from jax.sharding import PartitionSpec as P

limits = (12, 16, 23, 32, 45, 64, 91)


def passed_along(value, axis, steps):
    count = lax.axis_size(axis)
    pairs = [(source, (source + steps) % count) for source in range(count)]
    return lax.ppermute(value, axis, pairs)


def bucket_table(length):
    places = jnp.arange(length, dtype=jnp.int32)
    offset = places[None, :] - places[:, None]
    apart = jnp.abs(offset)
    bucket = jnp.minimum(apart, 8)
    for limit in limits:
        bucket = bucket + (apart >= limit).astype(jnp.int32)
    bucket = bucket + 16 * (offset > 0).astype(jnp.int32)
    return bucket


def attend_row(row_normed, row_segs, bias_full, heads, head_size):
    length = row_normed.shape[0]
    split = row_normed.reshape(length, heads, head_size).astype(jnp.float32)
    scores = jnp.einsum("qhd,khd->hqk", split, split) / head_size + bias_full
    same = row_segs[:, None] == row_segs[None, :]
    scores = jnp.where(same[None, :, :], scores, -1e30)
    top = jnp.max(scores, axis=-1, keepdims=True)
    expo = jnp.exp(scores - top)
    probs = (expo / jnp.sum(expo, axis=-1, keepdims=True)).astype(jnp.bfloat16)
    mixed = jnp.einsum("hqk,khd->qhd", probs.astype(jnp.float32), split)
    return mixed.reshape(length, heads * head_size)


def layer(embedded, gain, bias, segs):
    rows_count, length = segs.shape
    width = embedded.shape[1]
    heads = bias.shape[1]
    head_size = width // heads
    wide = embedded.astype(jnp.float32)
    meansq = jnp.mean(wide * wide, axis=-1, keepdims=True)
    normed = (wide * lax.rsqrt(meansq + 1e-06) * gain).astype(jnp.bfloat16)
    picks = (bucket_table(length)[:, :, None] == jnp.arange(bias.shape[0], dtype=jnp.int32)).astype(
        jnp.float32
    )
    bias_full = jnp.einsum("qkb,bh->hqk", picks, bias)
    blocks = normed.reshape(rows_count, length, width)
    mixed = jax.vmap(
        lambda row_block, row_segs: attend_row(row_block, row_segs, bias_full, heads, head_size)
    )(blocks, segs)
    return (wide + mixed.reshape(rows_count * length, width)).astype(jnp.bfloat16)


def local(token_ids, segment_ids, row_order, embed_table, norm_gain, position_bias, returned_grad):
    all_ids, all_segs = (
        lax.all_gather(token_ids[0], "dp", axis=0, tiled=True),
        lax.all_gather(segment_ids[0], "dp", axis=0, tiled=True),
    )
    order = row_order[0]
    packed = jnp.take(all_ids, order, axis=0)
    row_segs = jnp.take(all_segs, order, axis=0)
    vocab = embed_table.shape[1]
    onehot = (packed.reshape(-1)[:, None] == jnp.arange(vocab, dtype=jnp.int32)[None, :]).astype(
        jnp.bfloat16
    )
    embedded = jnp.dot(onehot, embed_table[0], preferred_element_type=jnp.float32).astype(
        jnp.bfloat16
    )
    result, pullback = jax.vjp(
        lambda first, second, third: layer(first, second, third, row_segs),
        embedded,
        norm_gain[0],
        position_bias[0],
    )
    handed = passed_along(result, "section", 1)
    incoming = passed_along(returned_grad[0], "section", -1)
    grad_rows, grad_g, grad_b = pullback(incoming)
    table_term = lax.dot_general(
        onehot, grad_rows, (((0,), (0,)), ((), ())), preferred_element_type=jnp.float32
    )
    grad_tab = lax.psum_scatter(table_term, "dp", scatter_dimension=0, tiled=True)
    grad_g, grad_b = lax.psum((grad_g, grad_b), "dp")
    return (handed[None], grad_tab[None], grad_g[None], grad_b[None])


def solution(mesh):
    placed = (
        P("section", "dp", None),
        P("section", "dp", None),
        P("section", "dp"),
        P("section", None, None),
        P("section", None),
        P("section", None, None),
        P("section", "dp", None),
    )
    return jax.shard_map(
        local,
        mesh=mesh,
        in_specs=placed,
        out_specs=(
            P("section", "dp", None),
            P("section", "dp", None),
            P("section", None),
            P("section", None, None),
        ),
        check_vma=False,
    )
```

profile of v0, /device:TPU:24, one launch (start us, length us, event | category | flops | bytes accessed | tf_op | source)
XLA Modules:
  0.0 409.5 jit_solution(6703125069498743781)
XLA Ops:
  7.2 0.0 copy-start
  7.2 0.0 copy-start.8
  7.2 0.0 all-reduce.4.cloned.1.call-start
  7.2 0.8 collective-permute-start.1
  8.1 0.1 select_add_fusion
  8.8 42.7 %all-gather = s32[64,1,128]{2,1,0:T(1,128)S(1)} all-gather(s32[1,1,128]{2,1,0:T(1,128)} %param.9), channel_id=2, replica_groups=mesh['dp'=64,'section'=4] {'dp'}, dimensions={0}, use_global_device_ids=true | all-gather | bytes 33280 | tf_op jit(solution)/shard_map/all_gather | solution.py:60
  51.5 0.0 copy-start.7
  51.5 3.0 multiply_reduce_fusion.2
  54.5 0.0 copy-done.8
  54.5 37.3 %all-gather.1 = s32[64,1,128]{2,1,0:T(1,128)S(1)} all-gather(s32[1,1,128]{2,1,0:T(1,128)S(1)} %copy-done.8), channel_id=3, replica_groups=mesh['dp'=64,'section'=4] {'dp'}, dimensions={0}, use_global_device_ids=true | all-gather | bytes 33280 | tf_op jit(solution)/shard_map/all_gather | solution.py:61
  91.9 0.0 copy-done
  91.9 2.7 fusion.17
  94.6 0.0 copy-done.7
  94.6 1.2 multiply_convert_fusion
  95.8 0.1 broadcast_compare_fusion.1
  95.9 1.6 copy.37
  97.5 5.4 %copy.38 = f32[128,128,64]{0,1,2:T(8,128)} copy(f32[128,128,64]{1,2,0:T(8,128)} %fusion.17) | data formatting | bytes 8388608 | tf_op jit(solution)/shard_map/jvp(qkb,bh->hqk)/dot_general | solution.py:50
  102.9 3.3 fusion.47
  106.2 0.0 copy-start.2
  106.2 1.9 copy-done.2
  108.1 0.9 fusion.13
  109.1 0.0 collective-permute-done.1
  109.1 2.3 copy.41
  111.4 0.0 copy-start.3
  111.4 4.1 fusion.6
  115.4 0.0 copy-done.3
  115.5 2.6 convert_reduce_fusion
  118.0 2.2 add_select_fusion
  120.2 0.0 copy-start.4
  120.2 1.5 fusion.11
  121.8 0.7 fusion.9
  122.4 0.0 copy-done.4
  122.4 0.0 copy-start.6
  122.5 2.0 fusion.50
  124.4 0.0 copy-done.6
  124.4 1.5 fusion.15
  126.0 1.5 bitcast_convert_fusion
  127.5 2.9 copy.45
  130.4 2.9 copy.40
  133.3 0.0 copy-start.5
  133.3 4.0 multiply_reduce_fusion
  137.4 0.0 copy-done.5
  137.4 5.9 %fusion.21 = f32[512,4096]{1,0:T(8,128)} fusion(f32[128,4096]{1,0:T(8,128)S(1)} %get-tuple-element.27, bf16[128,4096]{1,0:T(8,128)(2,1)} %collective-permute-done.1, f32[128,4096]{1,0:T(8,128)S(1)} %copy-done.5, f32[128]{0:T(128)S(1)} %multiply_multiply_fusion, f32[4096]{0:T(1024)S(1)} %bitcast.114, f32[128]{0:T(128)S(1)} %fusion.42, s32[128]{0:T(128)S(1)} %fusion.40), kind=kOutput, calls=%fused_computation.40 | convolution fusion | flops 541130752 | bytes 13649408 | tf_op jit(solution)/shard_map/dot_general | solution.py:82
  143.3 0.0 copy-start.9
  143.3 0.0 all-reduce.4.cloned.1.call-update
  143.3 2.6 collective-permute-start
  145.9 0.0 copy-done.9
  145.9 0.6 dynamic-slice.7
  146.4 0.0 copy-start.1
  147.1 4.1 copy.47
  151.2 0.7 fusion.20
  151.9 248.2 %all-reduce.1 = (f32[1,4096]{1,0:T(1,128)}, f32[1,32,64]{2,1,0:T(8,128)}) all-reduce(f32[1,4096]{1,0:T(1,128)S(1)} %bitcast.115, f32[1,32,64]{2,1,0:T(8,128)S(1)} %fusion.20), channel_id=1, replica_groups=mesh['dp'=64,'section'=4] {'dp'}, use_global_device_ids=true, to_apply=%region_9.11 | all-reduce | flops 6144 | bytes 49152 | tf_op jit(solution)/shard_map/psum | solution.py:86
  400.1 0.0 collective-permute-done
  400.1 0.0 all-reduce.4.cloned.1.call-done
  400.1 1.6 dynamic-slice_bitcast_fusion
  401.7 1.0 copy.55
  402.6 0.0 copy-done.1
  (7 shorter events, 0.1 us)
Async XLA Ops:
  7.2 84.7 %copy-start = (f32[1,32,64]{2,1,0:T(8,128)S(1)}, f32[1,32,64]{2,1,0:T(8,128)}, u32[]{:S(2)}) copy-start(f32[1,32,64]{2,1,0:T(8,128)} %param.14) | copy-start | bytes 24580
  7.2 47.3 %copy-start.8 = (s32[1,1,128]{2,1,0:T(1,128)S(1)}, s32[1,1,128]{2,1,0:T(1,128)}, u32[]{:S(2)}) copy-start(s32[1,1,128]{2,1,0:T(1,128)} %param.10) | copy-start | bytes 1540
  7.2 392.9 %all-reduce.4.cloned.1.call-start = ((), (), s32[]{:S(2)}) async-start(), calls=%async_computation | async-start | bytes 16777216
  7.2 101.9 %collective-permute-start.1 = (bf16[128,4096]{1,0:T(8,128)(2,1)}, bf16[128,4096]{1,0:T(8,128)(2,1)}, u32[]{:S(2)}, u32[]{:S(2)}) collective-permute-start(bf16[128,4096]{1,0:T(8,128)(2,1)} %bitcast.118), channel_id=1, source_target_pairs={{0,3},{1,0},{2,1},{3,2},{4,7},{5,4},{6,5},{7,6},{8,11},{9,8},{10,9... | collective-permute-start | bytes 3145736 | tf_op jit(solution)/shard_map/ppermute | solution.py:12
  51.5 43.1 %copy-start.7 = (f32[1,4096]{1,0:T(1,128)S(1)}, f32[1,4096]{1,0:T(1,128)}, u32[]{:S(2)}) copy-start(f32[1,4096]{1,0:T(1,128)} %param.13) | copy-start | bytes 49156
  106.2 1.9 copy-start.2
  111.4 4.1 copy-start.3
  120.2 2.2 copy-start.4
  122.4 2.0 copy-start.6
  133.3 4.0 copy-start.5
  143.3 2.6 copy-start.9
  143.3 256.8 %collective-permute-start = (bf16[128,4096]{1,0:T(8,128)(2,1)}, bf16[128,4096]{1,0:T(8,128)(2,1)S(1)}, u32[]{:S(2)}, u32[]{:S(2)}) collective-permute-start(bf16[128,4096]{1,0:T(8,128)(2,1)} %get-tuple-element.25), channel_id=1, source_target_pairs={{0,1},{1,2},{2,3},{3,0},{4,5},{5,6},{6,7},{7,4},{8,9},{9,10},{10,1... | collective-permute-start | bytes 3145736 | tf_op jit(solution)/shard_map/ppermute | solution.py:12
  146.4 256.2 %copy-start.1 = (f32[1,32,64]{2,1,0:T(8,128)S(1)}, f32[1,32,64]{2,1,0:T(8,128)}, u32[]{:S(2)}) copy-start(f32[1,32,64]{2,1,0:T(8,128)} %param.14) | copy-start | bytes 24580
Sparse Core Ops, SparseCore 0:
  143.4 203.3 all-reduce.3
where the time goes:
time: 410 us; the launch traced here: 409 us
  blocking collectives  328 us (80%)
  matrix products  25.3 us (6%)
  local copies, waits for them, and re-layouts  24.3 us (6%)
  between operations  15.5 us (4%)
  other arithmetic  12.7 us (3%)
    psum x1, blocking collectives, local(): grad_g, grad_b = lax.psum((grad_g, grad_b), 'dp')  248 us
    all_gather x1, blocking collectives, local(): lax.all_gather(token_ids[0], 'dp', axis=0, tiled=True)  42.7 us
    all_gather x1, blocking collectives, local(): lax.all_gather(segment_ids[0], 'dp', axis=0, tiled=True)  37.3 us
  transfers between devices with their start and end apart: 3, of which 0 were waited for; matrix products, arithmetic and copies ran while one was open for 6% of the time, Pallas kernels for 0%

commit v1 on v0

--- a/solution.py
+++ b/solution.py
@@ -4,6 +4,13 @@
 from jax.sharding import PartitionSpec as P
 
 limits = (12, 16, 23, 32, 45, 64, 91)
+
+
+def swapped_in(x, name, d):
+    size = lax.axis_size(name)
+    blocks = jnp.stack([x for _ in range(size)])
+    blocks = lax.all_to_all(blocks, name, split_axis=0, concat_axis=0)
+    return jnp.concatenate(blocks, axis=d)
 
 
 def passed_along(value, axis, steps):
@@ -58,7 +65,7 @@
 def local(token_ids, segment_ids, row_order, embed_table, norm_gain, position_bias, returned_grad):
     all_ids, all_segs = (
         lax.all_gather(token_ids[0], "dp", axis=0, tiled=True),
-        lax.all_gather(segment_ids[0], "dp", axis=0, tiled=True),
+        swapped_in(segment_ids[0], "dp", 0),
     )
     order = row_order[0]
     packed = jnp.take(all_ids, order, axis=0)

time: 410 us -> 384 us (0.937)
  blocking collectives: 328 us -> 288 us
  starting transfers between devices: 3.43 us -> 15.4 us
    all_gather x1 -> x0, blocking collectives: 37.3 us -> none  [local(): lax.all_gather(segment_ids[0], 'dp', axis=0, tiled=True)]
    all_to_all x0 -> x1, starting transfers between devices: none -> 11.9 us  [swapped_in(): blocks = lax.all_to_all(blocks, name, split_axis=0, concat_axis=0)]
  transfers between devices with their start and end apart: 3 -> 4, of which waited for: 0 -> 0; matrix products, arithmetic and copies ran while one was open for 6% -> 6% of each run, Pallas kernels for 0% -> 0%
where the time goes in v1:
time: 384 us; the launch traced here: 383 us
  blocking collectives  288 us (75%)
  local copies, waits for them, and re-layouts  25.6 us (7%)
  matrix products  25.3 us (7%)
  between operations  15.5 us (4%)
  starting transfers between devices  15.4 us (4%)
  other arithmetic  12.7 us (3%)
    psum x1, blocking collectives, local(): grad_g, grad_b = lax.psum((grad_g, grad_b), 'dp')  247 us
    all_gather x1, blocking collectives, local(): lax.all_gather(token_ids[0], 'dp', axis=0, tiled=True)  41 us
    all_to_all x1, starting transfers between devices, swapped_in(): blocks = lax.all_to_all(blocks, name, split_axis=0, concat_axis=0)  11.9 us
  transfers between devices with their start and end apart: 4, of which 0 were waited for; matrix products, arithmetic and copies ran while one was open for 6% of the time, Pallas kernels for 0%

profile of v1, /device:TPU:24, one launch (start us, length us, event | category | flops | bytes accessed | tf_op | source)
XLA Modules:
  0.0 382.9 jit_solution(3658364714003314033)
XLA Ops:
  7.2 0.0 copy-start
  7.2 0.0 copy-start.7
  7.2 1.3 stack.3
  8.5 11.9 %all-to-all-start = ((s32[64,1,128]{2,1,0:T(1,128)}), s32[64,1,128]{2,1,0:T(1,128)S(1)}, u32[]{:S(2)}, u32[]{:S(2)}) async-start(s32[64,1,128]{2,1,0:T(1,128)} %stack.3), calls=%async_computation | async-start | bytes 65536 | tf_op jit(solution)/shard_map/all_to_all | solution.py:12
  20.4 0.0 all-reduce.4.cloned.1.call-start
  20.5 0.8 collective-permute-start.1
  21.3 0.1 select_add_fusion
  22.0 41.0 %all-gather = s32[64,1,128]{2,1,0:T(1,128)S(1)} all-gather(s32[1,1,128]{2,1,0:T(1,128)} %param.9), channel_id=2, replica_groups=mesh['dp'=64,'section'=4] {'dp'}, dimensions={0}, use_global_device_ids=true | all-gather | bytes 33280 | tf_op jit(solution)/shard_map/all_gather | solution.py:67
  63.0 3.0 multiply_reduce_fusion.2
  66.1 0.0 copy-done.7
  66.1 1.3 multiply_convert_fusion
  67.4 0.0 copy-done
  67.4 2.7 fusion.17
  70.0 1.6 copy.37
  71.7 5.4 %copy.38 = f32[128,128,64]{0,1,2:T(8,128)} copy(f32[128,128,64]{1,2,0:T(8,128)} %fusion.17) | data formatting | bytes 8388608 | tf_op jit(solution)/shard_map/jvp(qkb,bh->hqk)/dot_general | solution.py:57
  77.1 0.0 all-to-all-done
  77.1 0.1 broadcast_compare_fusion.1
  77.2 3.3 fusion.47
  80.4 0.0 copy-start.2
  80.5 1.9 copy-done.2
  82.4 0.9 fusion.13
  83.3 0.0 collective-permute-done.1
  83.3 2.3 copy.41
  85.6 0.0 copy-start.3
  85.6 4.1 %fusion.6 = (f32[64,128]{1,0:T(8,128)S(1)}, bf16[64,128,128]{2,1,0:T(8,128)(2,1)S(1)}) fusion(f32[64,128,128]{1,2,0:T(8,128)} %copy-done.2, f32[64,128]{1,0:T(8,128)S(1)} %multiply_divide_fusion, f32[64,128]{1,0:T(8,128)S(1)} %get-tuple-element.28, bf16[128,64,64]{0,2,1:T(8,128)(2,1)S(1)} %bitcast.105, bf16[64,64,128]{2,1,0:T(8,128)(2,1)} %bitcast.109), kind=kOutput, calls=%fused_computation.9 | convolution fusion | flops 140500992 | bytes 8486912 | tf_op jit(solution)/shard_map/transpose(jvp(vmap(hqk,khd->qhd)))/dot_general | solution.py:42
  89.7 0.0 copy-done.3
  89.7 2.6 convert_reduce_fusion
  92.3 2.2 add_select_fusion
  94.4 0.0 copy-start.4
  94.5 1.5 fusion.11
  96.0 0.7 fusion.9
  96.7 0.0 copy-done.4
  96.7 0.0 copy-start.6
  96.7 2.0 fusion.50
  98.7 0.0 copy-done.6
  98.7 1.5 fusion.15
  100.2 1.5 bitcast_convert_fusion
  101.8 2.9 copy.45
  104.7 2.9 copy.40
  107.6 0.0 copy-start.5
  107.6 4.0 %multiply_reduce_fusion = (f32[4096]{0:T(1024)S(1)}, f32[128]{0:T(128)S(1)}, bf16[128,4096]{1,0:T(8,128)(2,1)}) fusion(f32[128,4096]{1,0:T(8,128)} %copy.45, f32[128,4096]{1,0:T(8,128)S(1)} %get-tuple-element.27, f32[128]{0:T(128)S(1)} %fusion.42, f32[4096]{0:T(1024)S(1)} %bitcast.114, f32[128,4096]{1,0:T(8,128)} %copy.40), kind=kLoop, calls=%fused_computation.27 | loop fusion | flops 4190080 | bytes 7373824 | tf_op jit(solution)/shard_map/transpose(jvp())/reduce_sum | solution.py:53
  111.6 0.0 copy-done.5
  111.6 5.9 %fusion.21 = f32[512,4096]{1,0:T(8,128)} fusion(f32[128,4096]{1,0:T(8,128)S(1)} %get-tuple-element.27, bf16[128,4096]{1,0:T(8,128)(2,1)} %collective-permute-done.1, f32[128,4096]{1,0:T(8,128)S(1)} %copy-done.5, f32[128]{0:T(128)S(1)} %multiply_multiply_fusion, f32[4096]{0:T(1024)S(1)} %bitcast.115, f32[128]{0:T(128)S(1)} %fusion.42, s32[128]{0:T(128)S(1)} %fusion.40), kind=kOutput, calls=%fused_computation.40 | convolution fusion | flops 541130752 | bytes 13649408 | tf_op jit(solution)/shard_map/dot_general | solution.py:89
  117.5 0.0 copy-start.8
  117.5 0.0 all-reduce.4.cloned.1.call-update
  117.5 2.6 collective-permute-start
  120.1 0.0 copy-done.8
  120.1 0.6 dynamic-slice.7
  120.7 0.0 copy-start.1
  121.3 4.1 %copy.47 = bf16[64,128,128]{2,0,1:T(8,128)(2,1)S(1)} copy(f32[64,128,128]{1,2,0:T(8,128)} %copy-done.4) | data formatting | bytes 6291456 | tf_op jit(solution)/shard_map/transpose(jvp(vmap(jit(_where))))/select_n | solution.py:38
  125.4 0.7 fusion.20
  126.1 247.4 %all-reduce.1 = (f32[1,4096]{1,0:T(1,128)}, f32[1,32,64]{2,1,0:T(8,128)}) all-reduce(f32[1,4096]{1,0:T(1,128)S(1)} %bitcast.116, f32[1,32,64]{2,1,0:T(8,128)S(1)} %fusion.20), channel_id=1, replica_groups=mesh['dp'=64,'section'=4] {'dp'}, use_global_device_ids=true, to_apply=%region_9.11 | all-reduce | flops 6144 | bytes 49152 | tf_op jit(solution)/shard_map/psum | solution.py:93
  373.5 0.0 collective-permute-done
  373.5 0.0 all-reduce.4.cloned.1.call-done
  373.5 1.6 dynamic-slice_bitcast_fusion
  375.1 1.0 copy.55
  376.0 0.0 copy-done.1
  (7 shorter events, 0.1 us)
Async XLA Ops:
  7.2 60.2 %copy-start = (f32[1,32,64]{2,1,0:T(8,128)S(1)}, f32[1,32,64]{2,1,0:T(8,128)}, u32[]{:S(2)}) copy-start(f32[1,32,64]{2,1,0:T(8,128)} %param.14) | copy-start | bytes 24580
  7.2 58.9 %copy-start.7 = (f32[1,4096]{1,0:T(1,128)S(1)}, f32[1,4096]{1,0:T(1,128)}, u32[]{:S(2)}) copy-start(f32[1,4096]{1,0:T(1,128)} %param.13) | copy-start | bytes 49156
  8.5 68.6 %all-to-all-start = ((s32[64,1,128]{2,1,0:T(1,128)}), s32[64,1,128]{2,1,0:T(1,128)S(1)}, u32[]{:S(2)}, u32[]{:S(2)}) async-start(s32[64,1,128]{2,1,0:T(1,128)} %stack.3), calls=%async_computation | async-start | bytes 65536 | tf_op jit(solution)/shard_map/all_to_all | solution.py:12
  20.4 353.1 %all-reduce.4.cloned.1.call-start = ((), (), s32[]{:S(2)}) async-start(), calls=%async_computation.1 | async-start | bytes 16777216
  20.5 62.9 %collective-permute-start.1 = (bf16[128,4096]{1,0:T(8,128)(2,1)}, bf16[128,4096]{1,0:T(8,128)(2,1)}, u32[]{:S(2)}, u32[]{:S(2)}) collective-permute-start(bf16[128,4096]{1,0:T(8,128)(2,1)} %bitcast.120), channel_id=1, source_target_pairs={{0,3},{1,0},{2,1},{3,2},{4,7},{5,4},{6,5},{7,6},{8,11},{9,8},{10,9... | collective-permute-start | bytes 3145736 | tf_op jit(solution)/shard_map/ppermute | solution.py:19
  80.4 1.9 copy-start.2
  85.6 4.1 %copy-start.3 = (f32[64,128,128]{1,2,0:T(8,128)S(1)}, f32[64,128,128]{1,2,0:T(8,128)}, u32[]{:S(2)}) copy-start(f32[64,128,128]{1,2,0:T(8,128)} %copy-done.2) | copy-start | bytes 12582916
  94.4 2.2 copy-start.4
  96.7 2.0 copy-start.6
  107.6 4.0 %copy-start.5 = (f32[128,4096]{1,0:T(8,128)S(1)}, f32[128,4096]{1,0:T(8,128)}, u32[]{:S(2)}) copy-start(f32[128,4096]{1,0:T(8,128)} %copy.45) | copy-start | bytes 6291460
  117.5 2.6 copy-start.8
  117.5 256.0 %collective-permute-start = (bf16[128,4096]{1,0:T(8,128)(2,1)}, bf16[128,4096]{1,0:T(8,128)(2,1)S(1)}, u32[]{:S(2)}, u32[]{:S(2)}) collective-permute-start(bf16[128,4096]{1,0:T(8,128)(2,1)} %get-tuple-element.25), channel_id=1, source_target_pairs={{0,1},{1,2},{2,3},{3,0},{4,5},{5,6},{6,7},{7,4},{8,9},{9,10},{10,1... | collective-permute-start | bytes 3145736 | tf_op jit(solution)/shard_map/ppermute | solution.py:19
  120.7 255.4 %copy-start.1 = (f32[1,32,64]{2,1,0:T(8,128)S(1)}, f32[1,32,64]{2,1,0:T(8,128)}, u32[]{:S(2)}) copy-start(f32[1,32,64]{2,1,0:T(8,128)} %param.14) | copy-start | bytes 24580
Sparse Core Ops, SparseCore 0:
  117.6 203.1 all-reduce.3
